TPU v7x, 32 devices: a whole 2x2x4 slice. The times are simulated.
32 devices in a mesh: dp: 16 (over z, y, x), tensor: 2 (over core).
Axes of the slice: x: 2, y: 2, z: 4, core: 2. Of those that a mesh axis runs over, the one named last changes fastest.
Arguments:
- tokens: bfloat16 [2, 16, 256, 768], P(None, 'dp', 'tensor'), may hold values from -6 to 6
- lengths: int32 [2, 16, 8], P(None, 'dp'), may hold values from 1 to 64, 256 in all within a row
- qkv_weight: bfloat16 [2, 3, 768, 768], P(None, None, 'dp', 'tensor'), may hold values from -0.21875 to 0.21875
- qkv_bias: bfloat16 [2, 2, 2, 384], P(None, None, 'tensor', 'dp'), may hold values from -3 to 3
- out_weight: bfloat16 [2, 768, 768], P(None, 'tensor', 'dp'), may hold values from -0.875 to 0.875
- up_weight: bfloat16 [2, 768, 3072], P(None, 'dp', 'tensor'), may hold values from -0.21875 to 0.21875
- up_bias: bfloat16 [2, 2, 1536], P(None, 'tensor', 'dp'), may hold values from -3 to 3
- down_weight: bfloat16 [2, 3072, 768], P(None, 'tensor', 'dp'), may hold values from -0.109375 to 0.109375
- norm_gains: bfloat16 [2, 2, 768], P(None, None, 'dp'), may hold values from 0.5 to 1.5
- shifts: bfloat16 [2, 4, 768], P(None, None, 'dp'), may hold values from -2 to 2
- cotangent: bfloat16 [2, 16, 256, 768], P(None, 'dp', 'tensor'), may hold values from -6 to 6
Outputs:
- out_tokens: float32 [2, 16, 256, 768], P(None, 'dp', 'tensor')
- token_grad: float32 [2, 16, 256, 768], P(None, 'dp', 'tensor')
- qkv_weight_grad: float32 [2, 3, 768, 768], P(None, None, 'dp', 'tensor')
- qkv_bias_grad: float32 [2, 2, 2, 384], P(None, None, 'tensor', 'dp')
- out_weight_grad: float32 [2, 768, 768], P(None, 'tensor', 'dp')
- up_weight_grad: float32 [2, 768, 3072], P(None, 'dp', 'tensor')
- up_bias_grad: float32 [2, 2, 1536], P(None, 'tensor', 'dp')
- down_weight_grad: float32 [2, 3072, 768], P(None, 'tensor', 'dp')
- gain_grad: float32 [2, 2, 768], P(None, None, 'dp')
- shift_grad: float32 [2, 4, 768], P(None, None, 'dp')
Inputs may be any that keep to these rules, and one draw needn't show every extreme that they name: The 8 lengths of a row sum to 256; in every row the longest is exactly 64.
All inputs are finite; a program needn't handle non-finite values.
Results may differ from a plain program's by a relative error of at most 0.025.
Values may be sent and summed in bfloat16 or wider, within the bound.
No kernel may reach another device: no remote copies, remote signals or barrier semaphores. Data moves between devices by JAX's collectives and lax.ppermute only.
A program may use at most 192 MiB of HBM per device.

v0:
```python
import jax
import jax.numpy as jnp
from jax import lax
from jax.sharding import PartitionSpec as P

HD = 64
LEN = 256
SQRT_HALF = 0.7071067811865476
DENSITY_SCALE = 0.3989422804014327


def fetch_each(layer_weights):
    return (
        lax.all_gather(layer_weights[0], "dp", axis=1, tiled=True),
        lax.all_gather(layer_weights[1], "dp", axis=2, tiled=True),
        lax.all_gather(layer_weights[2], "dp", axis=1, tiled=True),
        lax.all_gather(layer_weights[3], "dp", axis=0, tiled=True),
        lax.all_gather(layer_weights[4], "dp", axis=1, tiled=True),
        lax.all_gather(layer_weights[5], "dp", axis=1, tiled=True),
        lax.all_gather(layer_weights[6], "dp", axis=1, tiled=True),
        lax.all_gather(layer_weights[7], "dp", axis=1, tiled=True),
    )


def gather_rows(half_rows):
    return lax.all_gather(half_rows, "tensor", axis=0, tiled=True)


def sum_rows(term_fn, row_count):
    return lax.psum_scatter(
        term_fn(jnp.int32(0), row_count * lax.axis_size("tensor")).astype(jnp.bfloat16),
        "tensor",
        scatter_dimension=0,
        tiled=True,
    ).astype(jnp.float32)


def segment_ids(row_lengths):
    finish = jnp.cumsum(row_lengths, dtype=jnp.int32)
    places = jnp.arange(LEN, dtype=jnp.int32)
    return jnp.sum((places[:, None] >= finish[None, :]).astype(jnp.int32), axis=1, dtype=jnp.int32)


def gelu_value(widened):
    return 0.5 * widened * (1.0 + lax.erf(widened * SQRT_HALF))


def gelu_slope(widened):
    return (
        0.5 * (1.0 + lax.erf(widened * SQRT_HALF))
        + widened * jnp.exp(-0.5 * widened * widened) * DENSITY_SCALE
    )


def norm_forward(summed, gain, shift):
    center = summed - jnp.mean(summed, axis=-1, keepdims=True)
    spread = jnp.mean(center * center, axis=-1, keepdims=True)
    scaling = lax.rsqrt(spread + 1e-12)
    normal = center * scaling
    return (normal * gain.astype(jnp.float32) + shift, normal, scaling)


def norm_backward(upstream, normal, scaling, gain):
    gain_part = jnp.sum(upstream * normal, axis=0)
    shift_part = jnp.sum(upstream, axis=0)
    scaled = upstream * gain.astype(jnp.float32)
    centered = scaled - jnp.mean(scaled, axis=-1, keepdims=True)
    back = scaling * (centered - normal * jnp.mean(scaled * normal, axis=-1, keepdims=True))
    return (back, gain_part, shift_part)


def split_heads(projected):
    length = projected.shape[0]
    heads = projected.shape[2] // HD
    block = min(length, 512)
    blocks = length // block
    keys_all = projected[:, 1].reshape(length, heads, HD)
    values_all = projected[:, 2].reshape(length, heads, HD)
    queries = projected[:, 0].reshape(blocks, block, heads, HD)
    return (length, heads, block, blocks, queries, keys_all, values_all)


def attention(projected, segment):
    length, heads, block, blocks, queries, keys_all, values_all = split_heads(projected)

    def one_block(packed):
        query_block, segment_block = packed
        raw_scores = (
            jnp.einsum("qhd,khd->hqk", query_block, keys_all, preferred_element_type=jnp.float32)
            * 0.125
        )
        allowed = segment_block[:, None] == segment[None, :]
        scores = jnp.where(allowed[None], raw_scores, -1000000000.0)
        highest = jnp.max(scores, axis=-1, keepdims=True)
        raised = jnp.exp(scores - highest)
        row_total = jnp.sum(raised, axis=-1, keepdims=True)
        weights = (raised / row_total).astype(jnp.bfloat16)
        context = jnp.einsum(
            "hqk,khd->qhd", weights, values_all, preferred_element_type=jnp.float32
        )
        return (
            context.reshape(block, heads * HD).astype(jnp.bfloat16),
            (highest + jnp.log(row_total))[:, :, 0],
        )

    context, log_totals = lax.map(one_block, (queries, segment.reshape(blocks, block)))
    return (context.reshape(length, heads * HD), log_totals)


def attention_back(projected, segment, log_totals, context_grad):
    length, heads, block, blocks, queries, keys_all, values_all = split_heads(projected)
    grad_blocks = context_grad.reshape(blocks, block, heads, HD)

    def one_block(carry, packed):
        key_grad, value_grad = carry
        query_block, segment_block, log_block, grad_block = packed
        raw_scores = (
            jnp.einsum("qhd,khd->hqk", query_block, keys_all, preferred_element_type=jnp.float32)
            * 0.125
        )
        allowed = segment_block[:, None] == segment[None, :]
        scores = jnp.where(allowed[None], raw_scores, -1000000000.0)
        weights = jnp.exp(scores - log_block[:, :, None])
        value_grad = value_grad + jnp.einsum(
            "hqk,qhd->khd",
            weights.astype(jnp.bfloat16),
            grad_block,
            preferred_element_type=jnp.float32,
        )
        weight_grad = jnp.einsum(
            "qhd,khd->hqk", grad_block, values_all, preferred_element_type=jnp.float32
        )
        inner = jnp.sum(weights * weight_grad, axis=-1, keepdims=True)
        score_grad = (weights * (weight_grad - inner)).astype(jnp.bfloat16)
        query_grad = (
            jnp.einsum("hqk,khd->qhd", score_grad, keys_all, preferred_element_type=jnp.float32)
            * 0.125
        )
        key_grad = (
            key_grad
            + jnp.einsum(
                "hqk,qhd->khd", score_grad, query_block, preferred_element_type=jnp.float32
            )
            * 0.125
        )
        return ((key_grad, value_grad), query_grad.reshape(block, heads * HD).astype(jnp.bfloat16))

    start_zero = jnp.zeros((length, heads, HD), jnp.float32)
    (key_grad, value_grad), query_grad = lax.scan(
        one_block,
        (start_zero, start_zero),
        (queries, segment.reshape(blocks, block), log_totals, grad_blocks),
    )
    return jnp.stack(
        [
            query_grad.reshape(length, heads * HD),
            key_grad.reshape(length, heads * HD).astype(jnp.bfloat16),
            value_grad.reshape(length, heads * HD).astype(jnp.bfloat16),
        ],
        axis=1,
    )


def forward_layer(x_half, segment, layer_weights):
    (
        layer_qkv,
        layer_qkv_bias,
        layer_out,
        layer_up,
        layer_up_bias,
        layer_down,
        layer_gains,
        layer_shifts,
    ) = layer_weights
    half_rows = x_half.shape[0]
    entering = gather_rows(x_half.astype(jnp.bfloat16))
    projected = jnp.einsum("td,kdc->tkc", entering, layer_qkv, preferred_element_type=jnp.float32)
    bias_rows = layer_qkv_bias.reshape(2, -1).astype(jnp.float32)
    bias_all = jnp.stack([bias_rows[0], jnp.zeros_like(bias_rows[0]), bias_rows[1]])
    projected = (projected + bias_all).astype(jnp.bfloat16)
    context, log_totals = attention(projected, segment)

    def out_term(first_row, row_count):
        return jnp.dot(context, layer_out, preferred_element_type=jnp.float32)

    shift_rows = layer_shifts.astype(jnp.float32)
    first_sum = x_half + sum_rows(out_term, half_rows) + shift_rows[0]
    normed, normal_one, scale_one = norm_forward(first_sum, layer_gains[0], shift_rows[1])
    widened_in = gather_rows(normed.astype(jnp.bfloat16))
    widened = jnp.dot(
        widened_in, layer_up, preferred_element_type=jnp.float32
    ) + layer_up_bias.reshape(-1).astype(jnp.float32)
    activated = gelu_value(widened).astype(jnp.bfloat16)

    def down_term(first_row, row_count):
        return jnp.dot(activated, layer_down, preferred_element_type=jnp.float32)

    second_sum = normed + sum_rows(down_term, half_rows) + shift_rows[2]
    result, normal_two, scale_two = norm_forward(second_sum, layer_gains[1], shift_rows[3])
    stored = (
        entering,
        projected,
        context,
        log_totals,
        normal_one,
        scale_one,
        widened_in,
        widened,
        activated,
        normal_two,
        scale_two,
    )
    return (result, stored)


def backward_layer(upstream, segment, layer_weights, stored):
    (
        layer_qkv,
        layer_qkv_bias,
        layer_out,
        layer_up,
        layer_up_bias,
        layer_down,
        layer_gains,
        layer_shifts,
    ) = layer_weights
    (
        entering,
        projected,
        context,
        log_totals,
        normal_one,
        scale_one,
        widened_in,
        widened,
        activated,
        normal_two,
        scale_two,
    ) = stored
    half_rows = upstream.shape[0]
    second_grad, gain_two, shift_two = norm_backward(
        upstream, normal_two, scale_two, layer_gains[1]
    )
    down_seed = gather_rows(second_grad.astype(jnp.bfloat16))
    down_grad = jnp.einsum("tf,td->fd", activated, down_seed, preferred_element_type=jnp.float32)
    active_grad = jnp.einsum("td,fd->tf", down_seed, layer_down, preferred_element_type=jnp.float32)
    widened_grad = (active_grad * gelu_slope(widened)).astype(jnp.bfloat16)
    up_grad = jnp.einsum("td,tf->df", widened_in, widened_grad, preferred_element_type=jnp.float32)
    up_bias_grad = jnp.sum(widened_grad, axis=0, dtype=jnp.float32).reshape(1, -1)

    def up_term(first_row, row_count):
        return jnp.einsum("tf,df->td", widened_grad, layer_up, preferred_element_type=jnp.float32)

    normed_grad = second_grad + sum_rows(up_term, half_rows)
    first_grad, gain_one, shift_one = norm_backward(
        normed_grad, normal_one, scale_one, layer_gains[0]
    )
    out_seed = gather_rows(first_grad.astype(jnp.bfloat16))
    out_grad = jnp.einsum("tc,td->cd", context, out_seed, preferred_element_type=jnp.float32)
    context_grad = jnp.einsum(
        "td,cd->tc", out_seed, layer_out, preferred_element_type=jnp.float32
    ).astype(jnp.bfloat16)
    projected_grad = attention_back(projected, segment, log_totals, context_grad)
    column_sums = jnp.sum(projected_grad, axis=0, dtype=jnp.float32)
    qkv_bias_grad = jnp.stack([column_sums[0], column_sums[2]]).reshape(2, 1, -1)
    qkv_grad = jnp.einsum(
        "td,tkc->kdc", entering, projected_grad, preferred_element_type=jnp.float32
    )

    def in_term(first_row, row_count):
        return jnp.einsum(
            "tkc,kdc->td", projected_grad, layer_qkv, preferred_element_type=jnp.float32
        )

    input_grad = first_grad + sum_rows(in_term, half_rows)
    gain_grads = jnp.stack([gain_one, gain_two])
    shift_grads = jnp.stack(
        [jnp.sum(first_grad, axis=0), shift_one, jnp.sum(second_grad, axis=0), shift_two]
    )
    return (
        input_grad,
        (
            qkv_grad,
            qkv_bias_grad,
            out_grad,
            up_grad,
            up_bias_grad,
            down_grad,
            gain_grads,
            shift_grads,
        ),
    )


def on_device(
    tokens,
    lengths,
    qkv_weight,
    qkv_bias,
    out_weight,
    up_weight,
    up_bias,
    down_weight,
    norm_gains,
    shifts,
    cotangent,
):
    params = (qkv_weight, qkv_bias, out_weight, up_weight, up_bias, down_weight, norm_gains, shifts)
    layers = qkv_weight.shape[0]
    micro = tokens.shape[0]

    def layer_params(layer_index):
        return fetch_each(tuple((member[layer_index] for member in params)))

    totals = [None] * layers
    out_list = []
    grad_list = []
    for micro_index in range(micro):
        segment = segment_ids(lengths[micro_index, 0])
        hidden = tokens[micro_index, 0].astype(jnp.float32)
        stored_list = []
        for layer_index in range(layers):
            hidden, stored = forward_layer(hidden, segment, layer_params(layer_index))
            stored_list.append(stored)
        out_list.append(hidden)
        upstream = cotangent[micro_index, 0].astype(jnp.float32)
        for layer_index in reversed(range(layers)):
            upstream, layer_grads = backward_layer(
                upstream, segment, layer_params(layer_index), stored_list[layer_index]
            )
            share_part = (
                lax.psum_scatter(layer_grads[0], "dp", scatter_dimension=1, tiled=True),
                lax.psum_scatter(layer_grads[1], "dp", scatter_dimension=2, tiled=True),
                lax.psum_scatter(layer_grads[2], "dp", scatter_dimension=1, tiled=True),
                lax.psum_scatter(layer_grads[3], "dp", scatter_dimension=0, tiled=True),
                lax.psum_scatter(layer_grads[4], "dp", scatter_dimension=1, tiled=True),
                lax.psum_scatter(layer_grads[5], "dp", scatter_dimension=1, tiled=True),
                lax.psum_scatter(layer_grads[6], "dp", scatter_dimension=1, tiled=True),
                lax.psum_scatter(layer_grads[7], "dp", scatter_dimension=1, tiled=True),
            )
            totals[layer_index] = (
                share_part
                if totals[layer_index] is None
                else jax.tree.map(jnp.add, totals[layer_index], share_part)
            )
        grad_list.append(upstream)
    stacked = [
        jnp.stack([layer_total[member_index] for layer_total in totals])
        for member_index in range(8)
    ]
    gain_total, shift_total = lax.psum((stacked[6], stacked[7]), "tensor")
    return (
        jnp.stack(out_list)[:, None],
        jnp.stack(grad_list)[:, None],
        stacked[0],
        stacked[1],
        stacked[2],
        stacked[3],
        stacked[4],
        stacked[5],
        gain_total,
        shift_total,
    )


def solution(mesh):
    in_specs = (
        P(None, "dp", "tensor", None),
        P(None, "dp", None),
        P(None, None, "dp", "tensor"),
        P(None, None, "tensor", "dp"),
        P(None, "tensor", "dp"),
        P(None, "dp", "tensor"),
        P(None, "tensor", "dp"),
        P(None, "tensor", "dp"),
        P(None, None, "dp"),
        P(None, None, "dp"),
        P(None, "dp", "tensor", None),
    )
    out_specs = (
        P(None, "dp", "tensor", None),
        P(None, "dp", "tensor", None),
        P(None, None, "dp", "tensor"),
        P(None, None, "tensor", "dp"),
        P(None, "tensor", "dp"),
        P(None, "dp", "tensor"),
        P(None, "tensor", "dp"),
        P(None, "tensor", "dp"),
        P(None, None, "dp"),
        P(None, None, "dp"),
    )
    return jax.shard_map(
        on_device, mesh=mesh, in_specs=in_specs, out_specs=out_specs, check_vma=False
    )
```

profile of v0, /device:TPU:0, one launch (start us, length us, event | category | flops | bytes accessed | tf_op | source)
XLA Modules:
  0.0 2629.9 jit_solution(13975036079830027915)
XLA Ops:
  10.9 43.6 %all-gather.2 = bf16[1,2,1,384]{2,1,0,3:T(2,128)(2,1)S(1)} all-gather(bf16[1,2,1,24]{2,1,0,3:T(2,128)(2,1)S(1)} %copy.360), channel_id=4, replica_groups=mesh['dp'=16,'tensor'=2] {'dp'}, dimensions={3}, use_global_device_ids=true | all-gather | bytes 1632 | tf_op jit(solution)/shard_map/all_gather | solution.py:15
  56.3 37.4 %all-gather.10 = bf16[1,2,1,384]{2,1,0,3:T(2,128)(2,1)S(1)} all-gather(bf16[1,2,1,24]{2,1,0,3:T(2,128)(2,1)S(1)} %copy.363), channel_id=12, replica_groups=mesh['dp'=16,'tensor'=2] {'dp'}, dimensions={3}, use_global_device_ids=true | all-gather | bytes 1632 | tf_op jit(solution)/shard_map/all_gather | solution.py:15
  102.6 40.9 %all-gather.3 = bf16[1,384,768]{1,2,0:T(8,128)(2,1)S(1)} all-gather(bf16[1,384,48]{1,2,0:T(8,128)(2,1)S(1)} %get-tuple-element.417), channel_id=5, replica_groups=mesh['dp'=16,'tensor'=2] {'dp'}, dimensions={2}, use_global_device_ids=true | all-gather | bytes 626688 | tf_op jit(solution)/shard_map/all_gather | solution.py:16
  143.5 2.4 fusion.82
  166.8 38.0 %all-reduce.9 = (bf16[1536]{0:T(1024)(128)(2,1)S(1)}, bf16[1536]{0:T(1024)(128)(2,1)}) all-reduce(bf16[1536]{0:T(1024)(128)(2,1)S(1)} %dynamic-update-slice, bf16[1536]{0:T(1024)(128)(2,1)S(1)} %dynamic-update-slice.1), channel_id=9, replica_groups=mesh['dp'=16,'tensor'=2] {'dp'}, use_global_device_ids=true, to_apply=%add | all-reduce | flops 3072 | bytes 12288
  208.5 41.7 %all-gather.4 = bf16[1,4,768]{1,0,2:T(2,128)(2,1)S(1)} all-gather(bf16[1,4,48]{1,0,2:T(2,128)(2,1)} %copy.361), channel_id=6, replica_groups=mesh['dp'=16,'tensor'=2] {'dp'}, dimensions={2}, use_global_device_ids=true | all-gather | bytes 6528 | tf_op jit(solution)/shard_map/all_gather | solution.py:21
  250.5 39.1 %all-gather.5 = bf16[1,2,768]{1,0,2:T(2,128)(2,1)S(1)} all-gather(bf16[1,2,48]{1,0,2:T(2,128)(2,1)} %copy.362), channel_id=7, replica_groups=mesh['dp'=16,'tensor'=2] {'dp'}, dimensions={2}, use_global_device_ids=true | all-gather | bytes 3264 | tf_op jit(solution)/shard_map/all_gather | solution.py:20
  289.6 4.6 fusion.184
  294.3 11.0 slice_reduce_fusion.4
  313.5 3.6 convolution_add_fusion.5
  317.1 3.8 fusion.121
  323.3 4.0 multiply_convert_fusion.7
  330.5 44.5 %all-gather.11 = bf16[1,384,768]{1,2,0:T(8,128)(2,1)} all-gather(bf16[1,384,48]{1,2,0:T(8,128)(2,1)} %get-tuple-element.416), channel_id=13, replica_groups=mesh['dp'=16,'tensor'=2] {'dp'}, dimensions={2}, use_global_device_ids=true | all-gather | bytes 626688 | tf_op jit(solution)/shard_map/all_gather | solution.py:16
  382.2 19.3 all-gather.31.cloned.1.call-done
  420.9 2.6 fusion.252
  434.5 41.7 %all-gather.12 = bf16[1,4,768]{1,0,2:T(2,128)(2,1)S(1)} all-gather(bf16[1,4,48]{1,0,2:T(2,128)(2,1)} %copy.364), channel_id=14, replica_groups=mesh['dp'=16,'tensor'=2] {'dp'}, dimensions={2}, use_global_device_ids=true | all-gather | bytes 6528 | tf_op jit(solution)/shard_map/all_gather | solution.py:21
  476.6 40.0 %all-gather.13 = bf16[1,2,768]{1,0,2:T(2,128)(2,1)S(1)} all-gather(bf16[1,2,48]{1,0,2:T(2,128)(2,1)} %copy.365), channel_id=15, replica_groups=mesh['dp'=16,'tensor'=2] {'dp'}, dimensions={2}, use_global_device_ids=true | all-gather | bytes 3264 | tf_op jit(solution)/shard_map/all_gather | solution.py:20
  516.7 4.6 fusion.182
  521.3 11.5 slice_reduce_fusion
  538.4 3.7 convolution_add_fusion.4
  542.0 30.6 %all-gather.35.cloned.1.call-done = bf16[1,1536,768]{1,2,0:T(8,128)(2,1)} async-done(((bf16[1,1536,48]{1,2,0:T(8,128)(2,1)}), bf16[1,1536,768]{1,2,0:T(8,128)(2,1)}) %all-gather.35.cloned.1.call-update) | async-done | bytes 2359312 | tf_op jit(solution)/shard_map/all_gather | solution.py:19
  572.7 3.8 fusion.133
  578.8 3.9 multiply_convert_fusion.6
  586.5 7.9 reduce-scatter.49.cloned.1.call-done
  605.4 2.3 all_gather.156
  607.7 3.9 convert_reduce_fusion.1
  618.5 7.0 reduce-scatter.59.cloned.1.call-done
  625.5 3.4 fusion.219
  636.3 2.7 convolution_convert_fusion.10
  647.1 2.6 convolution_convert_fusion.6
  660.1 3.2 fusion.100
  673.3 3.3 fusion.103
  679.7 5.9 reduce-scatter.61.cloned.1.call-done
  685.7 2.6 fusion.217
  697.0 2.3 all_gather.162
  699.3 3.9 convert_reduce_fusion.2
  737.4 2.7 multiply_reduce_fusion.9
  742.8 2.5 all_gather.163
  766.6 3.0 fusion.109
  776.8 2.4 add_bitcast_fusion
  779.3 6.3 copy.318
  787.6 2.5 add_bitcast_fusion.1
  790.1 6.3 copy.315
  798.5 3.0 convolution_add_fusion.2
  803.6 3.0 convolution_add_fusion.3
  808.7 3.1 convolution_add_fusion
  813.9 3.1 convolution_add_fusion.1
  819.5 27.4 %reduce-scatter.89.cloned.1.call-done = f32[96,1]{1,0:T(8,128)} async-done(((f32[1536,1]{1,0:T(8,128)}), f32[96,1]{1,0:T(8,128)}) %reduce-scatter.89.cloned.1.call-update) | async-done | bytes 400
  848.1 125.8 %reduce-scatter.93.cloned.1.call-done = f32[48,2]{1,0:T(8,128)} async-done(((f32[768,2]{1,0:T(8,128)}), f32[48,2]{1,0:T(8,128)}) %reduce-scatter.93.cloned.1.call-update) | async-done | bytes 400
  974.7 126.9 %reduce-scatter.87.cloned.1.call-done = f32[96,1]{1,0:T(8,128)} async-done(((f32[1536,1]{1,0:T(8,128)}), f32[96,1]{1,0:T(8,128)}) %reduce-scatter.87.cloned.1.call-update) | async-done | bytes 400
  1103.1 125.4 %reduce-scatter.97.cloned.1.call-done = f32[48,4]{1,0:T(8,128)} async-done(((f32[768,4]{1,0:T(8,128)}), f32[48,4]{1,0:T(8,128)}) %reduce-scatter.97.cloned.1.call-update) | async-done | bytes 784
  1229.6 40.4 %all-reduce.6 = (f32[2,1,384]{2,0,1:T(2,128)S(1)}, f32[2,1,384]{2,0,1:T(2,128)S(1)}) all-reduce(f32[2,1,384]{2,0,1:T(2,128)S(1)} %fusion.207, f32[2,1,384]{2,0,1:T(2,128)S(1)} %fusion.206), channel_id=55, replica_groups=mesh['dp'=16,'tensor'=2] {'dp'}, use_global_device_ids=true, to_apply=%region_73.74.clone | all-reduce | flops 1536 | bytes 12288
  1270.7 84.7 %reduce-scatter.91.cloned.1.call-done = f32[48,2]{1,0:T(8,128)} async-done(((f32[768,2]{1,0:T(8,128)}), f32[48,2]{1,0:T(8,128)}) %reduce-scatter.91.cloned.1.call-update) | async-done | bytes 400
  1356.3 126.1 %reduce-scatter.95.cloned.1.call-done = f32[48,4]{1,0:T(8,128)} async-done(((f32[768,4]{1,0:T(8,128)}), f32[48,4]{1,0:T(8,128)}) %reduce-scatter.95.cloned.1.call-update) | async-done | bytes 784
  1483.2 3.1 all-reduce.8
  1486.2 5.8 reduce-scatter.73.cloned.1.call-done
  1492.9 10.2 reduce-scatter.65.cloned.1.call-done
  1505.1 129.7 %reduce-scatter.77.cloned.1.call-done = f32[384,48]{0,1:T(8,128)} async-done(((f32[384,768]{0,1:T(8,128)}), f32[384,48]{0,1:T(8,128)}) %reduce-scatter.77.cloned.1.call-update) | async-done | bytes 73744 | tf_op jit(solution)/shard_map/reduce_scatter | solution.py:334
  1634.7 129.3 %reduce-scatter.75.cloned.1.call-done = f32[384,48]{0,1:T(8,128)} async-done(((f32[384,768]{0,1:T(8,128)}), f32[384,48]{0,1:T(8,128)}) %reduce-scatter.75.cloned.1.call-update) | async-done | bytes 73744 | tf_op jit(solution)/shard_map/reduce_scatter | solution.py:334
  1765.6 282.5 %all-reduce.12.cloned.1.call-done = (f32[3,768,384]{2,0,1:T(4,128)}, f32[3,768,384]{2,0,1:T(4,128)}) async-done(((f32[3,768,384]{2,0,1:T(4,128)}, f32[3,768,384]{2,0,1:T(4,128)}), (f32[3,768,384]{2,0,1:T(4,128)}, f32[3,768,384]{2,0,1:T(4,128)})) %all-reduce.12.cloned.1.call-update) | async-done | bytes 7077904
  2051.0 140.0 %reduce-scatter.81.cloned.1.call-done = f32[48,1536]{1,0:T(8,128)} async-done(((f32[768,1536]{1,0:T(8,128)}), f32[48,1536]{1,0:T(8,128)}) %reduce-scatter.81.cloned.1.call-update) | async-done | bytes 294928 | tf_op jit(solution)/shard_map/reduce_scatter | solution.py:335
  2191.0 143.5 %reduce-scatter.79.cloned.1.call-done = f32[48,1536]{1,0:T(8,128)} async-done(((f32[768,1536]{1,0:T(8,128)}), f32[48,1536]{1,0:T(8,128)}) %reduce-scatter.79.cloned.1.call-update) | async-done | bytes 294928 | tf_op jit(solution)/shard_map/reduce_scatter | solution.py:335
  2336.3 141.6 %reduce-scatter.85.cloned.1.call-done = f32[1536,48]{0,1:T(8,128)} async-done(((f32[1536,768]{0,1:T(8,128)}), f32[1536,48]{0,1:T(8,128)}) %reduce-scatter.85.cloned.1.call-update) | async-done | bytes 294928 | tf_op jit(solution)/shard_map/reduce_scatter | solution.py:337
  2477.9 143.3 %reduce-scatter.83.cloned.1.call-done = f32[1536,48]{0,1:T(8,128)} async-done(((f32[1536,768]{0,1:T(8,128)}), f32[1536,48]{0,1:T(8,128)}) %reduce-scatter.83.cloned.1.call-update) | async-done | bytes 294928 | tf_op jit(solution)/shard_map/reduce_scatter | solution.py:337
  (753 shorter events, 260.1 us)
Async XLA Ops:
  7.2 88.3 %copy-start.4 = (bf16[2,1,128,768]{3,2,1,0:T(8,128)(2,1)S(1)}, bf16[2,1,128,768]{3,2,1,0:T(8,128)(2,1)}, u32[]{:S(2)}) copy-start(bf16[2,1,128,768]{3,2,1,0:T(8,128)(2,1)} %param.11) | copy-start | bytes 1179652
  7.2 136.3 %all-gather.25.cloned.1.call-start = ((), (), s32[]{:S(2)}) async-start(), calls=%async_computation.44 | async-start | bytes 1880064 | tf_op jit(solution)/shard_map/all_gather | solution.py:14
  9.0 296.4 %reduce-scatter.43.cloned.1.call-start = ((), (), s32[]{:S(2)}) async-start(), calls=%async_computation.28 | async-start | bytes 589824 | tf_op jit(solution)/shard_map/reduce_scatter | solution.py:30
  93.7 8.3 copy-start.140
  97.6 50.7 %copy-start.93 = (bf16[1,1,256,768]{3,2,1,0:T(8,128)(2,1)}, bf16[1,1,256,768]{3,2,1,0:T(8,128)(2,1)S(1)}, u32[]{:S(2)}) copy-start(bf16[1,1,256,768]{3,2,1,0:T(8,128)(2,1)S(1)} %all-gather) | copy-start | bytes 1179652
  99.7 46.2 %copy-start.82 = (bf16[1,1,256,768]{3,2,1,0:T(8,128)(2,1)}, bf16[1,1,256,768]{3,2,1,0:T(8,128)(2,1)S(1)}, u32[]{:S(2)}) copy-start(bf16[1,1,256,768]{3,2,1,0:T(8,128)(2,1)S(1)} %all-gather.17) | copy-start | bytes 1179652
  143.5 9.1 copy-start.5
  153.8 153.2 %reduce-scatter.51.cloned.1.call-start = ((), (), s32[]{:S(2)}) async-start(), calls=%async_computation.32 | async-start | bytes 589824 | tf_op jit(solution)/shard_map/reduce_scatter | solution.py:30
  158.4 46.9 %copy-start.184 = (bf16[2,4,48]{2,1,0:T(4,128)(2,1)S(1)}, bf16[2,4,48]{2,1,0:T(4,128)(2,1)}, u32[]{:S(2)}) copy-start(bf16[2,4,48]{2,1,0:T(4,128)(2,1)} %param.20) | copy-start | bytes 2308
  160.3 153.2 %all-gather.27.cloned.1.call-start = ((), (), s32[]{:S(2)}) async-start(), calls=%async_computation.45 | async-start | bytes 2506752 | tf_op jit(solution)/shard_map/all_gather | solution.py:17
  162.1 155.1 %all-gather.29.cloned.1.call-start = ((), (), s32[]{:S(2)}) async-start(), calls=%async_computation.46 | async-start | bytes 2506752 | tf_op jit(solution)/shard_map/all_gather | solution.py:19
  163.8 211.2 %reduce-scatter.53.cloned.1.call-start = ((), (), s32[]{:S(2)}) async-start(), calls=%async_computation.33 | async-start | bytes 589824 | tf_op jit(solution)/shard_map/reduce_scatter | solution.py:30
  294.3 80.8 %copy-start.134 = (f32[768]{0:T(1024)}, f32[768]{0:T(1024)S(1)}, u32[]{:S(2)}) copy-start(f32[768]{0:T(1024)S(1)} %get-tuple-element.340) | copy-start | bytes 9220
  305.3 71.9 %copy-start.141 = (f32[768]{0:T(1024)}, f32[768]{0:T(1024)S(1)}, u32[]{:S(2)}) copy-start(f32[768]{0:T(1024)S(1)} %get-tuple-element.341) | copy-start | bytes 9220
  320.9 54.1 %reduce-scatter.45.cloned.1.call-start = ((), (), s32[]{:S(2)}) async-start(), calls=%async_computation.29 | async-start | bytes 589824 | tf_op jit(solution)/shard_map/reduce_scatter | solution.py:30
  329.7 71.8 %all-gather.31.cloned.1.call-start = ((), (), s32[]{:S(2)}) async-start(), calls=%async_computation.47 | async-start | bytes 1880064 | tf_op jit(solution)/shard_map/all_gather | solution.py:14
  330.5 202.4 %reduce-scatter.47.cloned.1.call-start = ((), (), s32[]{:S(2)}) async-start(), calls=%async_computation.30 | async-start | bytes 589824 | tf_op jit(solution)/shard_map/reduce_scatter | solution.py:30
  377.0 26.8 %copy-start.160 = (f32[128]{0:T(128)}, f32[128]{0:T(128)S(1)}, u32[]{:S(2)}) copy-start(f32[128]{0:T(128)S(1)} %broadcast_multiply_fusion.22) | copy-start | bytes 1540
  420.9 112.0 %reduce-scatter.55.cloned.1.call-start = ((), (), s32[]{:S(2)}) async-start(), calls=%async_computation.34 | async-start | bytes 589824 | tf_op jit(solution)/shard_map/reduce_scatter | solution.py:30
  430.5 107.9 %all-gather.33.cloned.1.call-start = ((), (), s32[]{:S(2)}) async-start(), calls=%async_computation.48 | async-start | bytes 2506752 | tf_op jit(solution)/shard_map/all_gather | solution.py:17
  431.2 141.5 %all-gather.35.cloned.1.call-start = ((), (), s32[]{:S(2)}) async-start(), calls=%async_computation.49 | async-start | bytes 2506752 | tf_op jit(solution)/shard_map/all_gather | solution.py:19
  431.8 154.7 %reduce-scatter.57.cloned.1.call-start = ((), (), s32[]{:S(2)}) async-start(), calls=%async_computation.35 | async-start | bytes 589824 | tf_op jit(solution)/shard_map/reduce_scatter | solution.py:30
  476.6 56.2 %copy-start.142 = (f32[768]{0:T(1024)S(1)}, f32[768]{0:T(1024)}, u32[]{:S(2)}) copy-start(f32[768]{0:T(1024)} %copy-done.141) | copy-start | bytes 9220
  576.5 18.0 reduce-scatter.49.cloned.1.call-start
  585.1 11.5 copy-start.143
  585.1 30.3 %reduce-scatter.67.cloned.1.call-start = ((), (), s32[]{:S(2)}) async-start(), calls=%async_computation.40 | async-start | bytes 589824 | tf_op jit(solution)/shard_map/reduce_scatter | solution.py:30
  605.3 20.1 reduce-scatter.59.cloned.1.call-start
  612.5 13.0 copy-start.165
  614.1 62.5 %reduce-scatter.69.cloned.1.call-start = ((), (), s32[]{:S(2)}) async-start(), calls=%async_computation.41 | async-start | bytes 589824 | tf_op jit(solution)/shard_map/reduce_scatter | solution.py:30
  663.4 22.2 reduce-scatter.61.cloned.1.call-start
  673.3 12.4 copy-start.161
  676.5 60.7 %reduce-scatter.63.cloned.1.call-start = ((), (), s32[]{:S(2)}) async-start(), calls=%async_computation.38 | async-start | bytes 589824 | tf_op jit(solution)/shard_map/reduce_scatter | solution.py:30
  696.9 40.4 %reduce-scatter.71.cloned.1.call-start = ((), (), s32[]{:S(2)}) async-start(), calls=%async_computation.42 | async-start | bytes 589824 | tf_op jit(solution)/shard_map/reduce_scatter | solution.py:30
  704.2 7.2 copy-start.152
  705.8 141.1 %reduce-scatter.89.cloned.1.call-start = ((), (), s32[]{:S(2)}) async-start(), calls=%async_computation.57 | async-start | bytes 835584
  713.9 259.9 %reduce-scatter.93.cloned.1.call-start = ((), (), s32[]{:S(2)}) async-start(), calls=%async_computation.59 | async-start | bytes 417792
  721.7 15.8 copy-start.135
  723.3 378.3 %reduce-scatter.87.cloned.1.call-start = ((), (), s32[]{:S(2)}) async-start(), calls=%async_computation.56 | async-start | bytes 835584
  727.8 500.7 %reduce-scatter.97.cloned.1.call-start = ((), (), s32[]{:S(2)}) async-start(), calls=%async_computation.61 | async-start | bytes 417792
  737.2 618.2 %reduce-scatter.91.cloned.1.call-start = ((), (), s32[]{:S(2)}) async-start(), calls=%async_computation.58 | async-start | bytes 417792
  757.1 725.3 %reduce-scatter.95.cloned.1.call-start = ((), (), s32[]{:S(2)}) async-start(), calls=%async_computation.60 | async-start | bytes 417792
  759.5 732.5 %reduce-scatter.73.cloned.1.call-start = ((), (), s32[]{:S(2)}) async-start(), calls=%async_computation.43 | async-start | bytes 589824 | tf_op jit(solution)/shard_map/reduce_scatter | solution.py:30
  763.3 739.9 %reduce-scatter.65.cloned.1.call-start = ((), (), s32[]{:S(2)}) async-start(), calls=%async_computation.39 | async-start | bytes 589824 | tf_op jit(solution)/shard_map/reduce_scatter | solution.py:30
  769.7 865.0 %reduce-scatter.77.cloned.1.call-start = ((), (), s32[]{:S(2)}) async-start(), calls=%async_computation.51 | async-start | bytes 1253376 | tf_op jit(solution)/shard_map/reduce_scatter | solution.py:334
  772.2 991.9 %reduce-scatter.75.cloned.1.call-start = ((), (), s32[]{:S(2)}) async-start(), calls=%async_computation.50 | async-start | bytes 1253376 | tf_op jit(solution)/shard_map/reduce_scatter | solution.py:334
  774.6 1273.5 %all-reduce.12.cloned.1.call-start = ((), (), s32[]{:S(2)}) async-start(), calls=%async_computation.62 | async-start | bytes 18874368
  796.5 1394.5 %reduce-scatter.81.cloned.1.call-start = ((), (), s32[]{:S(2)}) async-start(), calls=%async_computation.53 | async-start | bytes 5013504 | tf_op jit(solution)/shard_map/reduce_scatter | solution.py:335
  801.5 1532.9 %reduce-scatter.79.cloned.1.call-start = ((), (), s32[]{:S(2)}) async-start(), calls=%async_computation.52 | async-start | bytes 5013504 | tf_op jit(solution)/shard_map/reduce_scatter | solution.py:335
  806.7 1671.3 %reduce-scatter.85.cloned.1.call-start = ((), (), s32[]{:S(2)}) async-start(), calls=%async_computation.55 | async-start | bytes 5013504 | tf_op jit(solution)/shard_map/reduce_scatter | solution.py:337
  811.8 1809.4 %reduce-scatter.83.cloned.1.call-start = ((), (), s32[]{:S(2)}) async-start(), calls=%async_computation.54 | async-start | bytes 5013504 | tf_op jit(solution)/shard_map/reduce_scatter | solution.py:337
  817.0 30.8 %copy-start.46 = (bf16[256,1,384]{2,0,1:T(8,128)(2,1)S(1)}, bf16[256,1,384]{2,0,1:T(8,128)(2,1)}, u32[]{:S(2)}) copy-start(bf16[256,1,384]{2,0,1:T(8,128)(2,1)} %copy.291) | copy-start | bytes 589828
  817.0 30.7 %copy-start.47 = (bf16[256,1,384]{2,0,1:T(8,128)(2,1)S(1)}, bf16[256,1,384]{2,0,1:T(8,128)(2,1)}, u32[]{:S(2)}) copy-start(bf16[256,1,384]{2,0,1:T(8,128)(2,1)} %copy.289) | copy-start | bytes 589828
  817.0 30.7 %copy-start.48 = (bf16[256,1,384]{2,0,1:T(8,128)(2,1)S(1)}, bf16[256,1,384]{2,0,1:T(8,128)(2,1)}, u32[]{:S(2)}) copy-start(bf16[256,1,384]{2,0,1:T(8,128)(2,1)} %copy.290) | copy-start | bytes 589828
  817.0 30.8 %copy-start.68 = (bf16[256,1,384]{2,0,1:T(8,128)(2,1)S(1)}, bf16[256,1,384]{2,0,1:T(8,128)(2,1)}, u32[]{:S(2)}) copy-start(bf16[256,1,384]{2,0,1:T(8,128)(2,1)} %copy.305) | copy-start | bytes 589828
  817.0 30.8 %copy-start.70 = (bf16[256,1,384]{2,0,1:T(8,128)(2,1)S(1)}, bf16[256,1,384]{2,0,1:T(8,128)(2,1)}, u32[]{:S(2)}) copy-start(bf16[256,1,384]{2,0,1:T(8,128)(2,1)} %copy.303) | copy-start | bytes 589828
  817.1 30.8 %copy-start.72 = (bf16[256,1,384]{2,0,1:T(8,128)(2,1)S(1)}, bf16[256,1,384]{2,0,1:T(8,128)(2,1)}, u32[]{:S(2)}) copy-start(bf16[256,1,384]{2,0,1:T(8,128)(2,1)} %copy.304) | copy-start | bytes 589828
  817.1 412.2 %copy-start.75 = (bf16[256,1,384]{2,0,1:T(8,128)(2,1)S(1)}, bf16[256,1,384]{2,0,1:T(8,128)(2,1)}, u32[]{:S(2)}) copy-start(bf16[256,1,384]{2,0,1:T(8,128)(2,1)} %copy-done.73) | copy-start | bytes 589828
  817.1 412.2 %copy-start.78 = (bf16[256,1,384]{2,0,1:T(8,128)(2,1)S(1)}, bf16[256,1,384]{2,0,1:T(8,128)(2,1)}, u32[]{:S(2)}) copy-start(bf16[256,1,384]{2,0,1:T(8,128)(2,1)} %copy-done.76) | copy-start | bytes 589828
  817.1 412.2 %copy-start.81 = (bf16[256,1,384]{2,0,1:T(8,128)(2,1)S(1)}, bf16[256,1,384]{2,0,1:T(8,128)(2,1)}, u32[]{:S(2)}) copy-start(bf16[256,1,384]{2,0,1:T(8,128)(2,1)} %copy-done.79) | copy-start | bytes 589828
  818.6 410.9 %copy-start.50 = (bf16[256,1,384]{2,0,1:T(8,128)(2,1)S(1)}, bf16[256,1,384]{2,0,1:T(8,128)(2,1)}, u32[]{:S(2)}) copy-start(bf16[256,1,384]{2,0,1:T(8,128)(2,1)} %copy-done.49) | copy-start | bytes 589828
  818.6 410.9 %copy-start.52 = (bf16[256,1,384]{2,0,1:T(8,128)(2,1)S(1)}, bf16[256,1,384]{2,0,1:T(8,128)(2,1)}, u32[]{:S(2)}) copy-start(bf16[256,1,384]{2,0,1:T(8,128)(2,1)} %copy-done.51) | copy-start | bytes 589828
  818.6 410.9 %copy-start.54 = (bf16[256,1,384]{2,0,1:T(8,128)(2,1)S(1)}, bf16[256,1,384]{2,0,1:T(8,128)(2,1)}, u32[]{:S(2)}) copy-start(bf16[256,1,384]{2,0,1:T(8,128)(2,1)} %copy-done.53) | copy-start | bytes 589828
  819.5 672.5 %copy-start.34 = (f32[128,768]{1,0:T(8,128)S(1)}, f32[128,768]{1,0:T(8,128)}, u32[]{:S(2)}) copy-start(f32[128,768]{1,0:T(8,128)} %copy-done.33) | copy-start | bytes 1179652
  847.9 655.3 %copy-start.32 = (f32[128,768]{1,0:T(8,128)S(1)}, f32[128,768]{1,0:T(8,128)}, u32[]{:S(2)}) copy-start(f32[128,768]{1,0:T(8,128)} %get-tuple-element.362) | copy-start | bytes 1179652
  (167 other events, 395.2 us)
Sparse Core Ops, SparseCore 0:
  11.3 62.2 all-gather.24
  153.9 3.6 reduce-scatter.42
  160.4 9.0 reduce-scatter.50
  172.8 66.4 all-gather.26
  242.5 61.0 all-gather.28
  321.1 5.6 reduce-scatter.52
  329.8 8.6 reduce-scatter.44
  341.2 60.2 all-gather.30
  421.0 6.5 reduce-scatter.46
  430.6 8.5 reduce-scatter.54
  442.6 65.2 all-gather.32
  510.5 62.1 all-gather.34
  576.6 6.1 reduce-scatter.56
  585.5 8.9 reduce-scatter.48
  605.5 8.9 reduce-scatter.66
  616.5 8.9 reduce-scatter.58
  663.5 8.9 reduce-scatter.68
  676.7 8.9 reduce-scatter.60
  697.1 8.9 reduce-scatter.62
  708.1 8.9 reduce-scatter.70
  721.8 125.0 reduce-scatter.88
  851.5 122.2 reduce-scatter.92
  978.6 123.0 reduce-scatter.86
  1106.1 122.3 reduce-scatter.96
  1233.1 122.2 reduce-scatter.90
  1360.0 122.3 reduce-scatter.94
  1485.0 6.9 reduce-scatter.72
  1494.2 8.9 reduce-scatter.64
  1507.9 126.7 reduce-scatter.76
  1639.3 124.6 reduce-scatter.74
  1770.4 277.6 all-reduce.11
  2053.3 137.6 reduce-scatter.80
  2196.0 138.3 reduce-scatter.78
  2339.6 138.2 reduce-scatter.84
  2483.1 138.0 reduce-scatter.82
where the time goes:
time: 2640 us; the launch traced here: 2630 us
  waiting for transfers between devices  1820 us (69%)
  blocking collectives  446 us (17%)
  local copies, waits for them, and re-layouts  141 us (5%)
  matrix products  128 us (5%)
  other arithmetic  79.9 us (3%)
    unnamed x42, waiting for transfers between devices  901 us
    reduce_scatter x2, waiting for transfers between devices, on_device(): lax.psum_scatter(layer_grads[5], 'dp', scatter_dimension=1, tiled=True)  285 us
    reduce_scatter x2, waiting for transfers between devices, on_device(): lax.psum_scatter(layer_grads[3], 'dp', scatter_dimension=0, tiled=True)  283 us
    reduce_scatter x2, waiting for transfers between devices, on_device(): lax.psum_scatter(layer_grads[2], 'dp', scatter_dimension=1, tiled=True)  259 us
    all_gather x2, blocking collectives, fetch_each(): lax.all_gather(layer_weights[2], 'dp', axis=1, tiled=True)  85.4 us
    all_gather x2, blocking collectives, fetch_each(): lax.all_gather(layer_weights[7], 'dp', axis=1, tiled=True)  83.4 us
    all_gather x2, blocking collectives, fetch_each(): lax.all_gather(layer_weights[1], 'dp', axis=2, tiled=True)  81 us
    all_gather x2, blocking collectives, fetch_each(): lax.all_gather(layer_weights[6], 'dp', axis=1, tiled=True)  79.1 us
  transfers between devices with their start and end apart: 35, of which 20 were waited for; matrix products, arithmetic and copies ran while one was open for 9% of the time, Pallas kernels for 0%

commit v1 on v0

--- a/solution.py
+++ b/solution.py
@@ -9,11 +9,33 @@
 DENSITY_SCALE = 0.3989422804014327
 
 
+def laid_out(parts, dim):
+    lengths = list(parts.shape[1:])
+    lengths[dim] *= parts.shape[0]
+    return jnp.moveaxis(parts, 0, dim).reshape(lengths)
+
+
+def gather_around(shard, axis, dim):
+    size = lax.axis_size(axis)
+    pairs = [(i, (i + 1) % size) for i in range(size)]
+    back = [(b, a) for a, b in pairs]
+    lower, upper = ([], [])
+    for step in range(size - 1):
+        if step % 2 == 0:
+            lower.append(lax.ppermute(lower[-1] if lower else shard, axis, pairs))
+        else:
+            upper.append(lax.ppermute(upper[-1] if upper else shard, axis, back))
+    blocks = jnp.stack([*lower[::-1], shard, *upper])
+    shift = lax.axis_index(axis) - len(lower)
+    blocks = blocks[(jnp.arange(size) - shift) % size]
+    return laid_out(blocks, dim)
+
+
 def fetch_each(layer_weights):
     return (
         lax.all_gather(layer_weights[0], "dp", axis=1, tiled=True),
         lax.all_gather(layer_weights[1], "dp", axis=2, tiled=True),
-        lax.all_gather(layer_weights[2], "dp", axis=1, tiled=True),
+        gather_around(layer_weights[2], "dp", 1),
         lax.all_gather(layer_weights[3], "dp", axis=0, tiled=True),
         lax.all_gather(layer_weights[4], "dp", axis=1, tiled=True),
         lax.all_gather(layer_weights[5], "dp", axis=1, tiled=True),

time: 2640 us -> 2680 us (1.015)
  blocking collectives: 446 us -> 364 us
  starting transfers between devices: 1.62 us -> 78.5 us
  waiting for transfers between devices: 1820 us -> 1850 us
    all_gather x2 -> x0, blocking collectives: 85.4 us -> none  [fetch_each(): lax.all_gather(layer_weights[2], 'dp', axis=1, tiled=True)]
    ppermute x0 -> x30, starting transfers between devices: none -> 76.8 us  [the longest x14 76.6 us: gather_around(): upper.append(lax.ppermute(upper[-1] if upper else shard, axis, back))]
  transfers between devices with their start and end apart: 35 -> 65, of which waited for: 20 -> 39; matrix products, arithmetic and copies ran while one was open for 9% -> 9% of each run, Pallas kernels for 0% -> 0%
where the time goes in v1:
time: 2680 us; the launch traced here: 2670 us
  waiting for transfers between devices  1850 us (69%)
  blocking collectives  364 us (14%)
  local copies, waits for them, and re-layouts  149 us (6%)
  matrix products  123 us (5%)
  other arithmetic  79.3 us (3%)
  starting transfers between devices  78.5 us (3%)
    unnamed x42, waiting for transfers between devices  907 us
    reduce_scatter x2, waiting for transfers between devices, on_device(): lax.psum_scatter(layer_grads[5], 'dp', scatter_dimension=1, tiled=True)  285 us
    reduce_scatter x2, waiting for transfers between devices, on_device(): lax.psum_scatter(layer_grads[3], 'dp', scatter_dimension=0, tiled=True)  283 us
    reduce_scatter x2, waiting for transfers between devices, on_device(): lax.psum_scatter(layer_grads[2], 'dp', scatter_dimension=1, tiled=True)  259 us
    all_gather x2, blocking collectives, fetch_each(): lax.all_gather(layer_weights[1], 'dp', axis=2, tiled=True)  84.8 us
    all_gather x2, blocking collectives, fetch_each(): lax.all_gather(layer_weights[7], 'dp', axis=1, tiled=True)  82.3 us
    all_gather x2, blocking collectives, fetch_each(): lax.all_gather(layer_weights[6], 'dp', axis=1, tiled=True)  80.7 us
    unnamed x2, blocking collectives  78.3 us
  transfers between devices with their start and end apart: 65, of which 39 were waited for; matrix products, arithmetic and copies ran while one was open for 9% of the time, Pallas kernels for 0%

profile of v1, /device:TPU:0, one launch (start us, length us, event | category | flops | bytes accessed | tf_op | source)
XLA Modules:
  0.0 2666.8 jit_solution(2041251774721417736)
XLA Ops:
  8.0 7.0 collective-permute-start.8
  20.0 42.5 %all-gather.2 = bf16[1,2,1,384]{2,1,0,3:T(2,128)(2,1)S(1)} all-gather(bf16[1,2,1,24]{2,1,0,3:T(2,128)(2,1)S(1)} %copy.360), channel_id=4, replica_groups=mesh['dp'=16,'tensor'=2] {'dp'}, dimensions={3}, use_global_device_ids=true | all-gather | bytes 1632 | tf_op jit(solution)/shard_map/all_gather | solution.py:37
  64.4 42.3 %all-gather.9 = bf16[1,2,1,384]{2,1,0,3:T(2,128)(2,1)S(1)} all-gather(bf16[1,2,1,24]{2,1,0,3:T(2,128)(2,1)S(1)} %copy.363), channel_id=11, replica_groups=mesh['dp'=16,'tensor'=2] {'dp'}, dimensions={3}, use_global_device_ids=true | all-gather | bytes 1632 | tf_op jit(solution)/shard_map/all_gather | solution.py:37
  108.7 5.6 collective-permute-start.9
  116.0 5.9 collective-permute-start.10
  123.5 5.9 collective-permute-start.11
  131.1 6.0 collective-permute-start.12
  139.7 5.6 collective-permute-start.13
  147.5 5.6 collective-permute-start.14
  153.4 7.3 collective-permute-done.22
  180.6 37.9 %all-reduce.9 = (bf16[1536]{0:T(1024)(128)(2,1)S(1)}, bf16[1536]{0:T(1024)(128)(2,1)}) all-reduce(bf16[1536]{0:T(1024)(128)(2,1)S(1)} %dynamic-update-slice, bf16[1536]{0:T(1024)(128)(2,1)S(1)} %dynamic-update-slice.1), channel_id=8, replica_groups=mesh['dp'=16,'tensor'=2] {'dp'}, use_global_device_ids=true, to_apply=%add | all-reduce | flops 3072 | bytes 12288
  221.0 40.5 %all-gather.3 = bf16[1,4,768]{1,0,2:T(2,128)(2,1)S(1)} all-gather(bf16[1,4,48]{1,0,2:T(2,128)(2,1)S(1)} %copy.361), channel_id=5, replica_groups=mesh['dp'=16,'tensor'=2] {'dp'}, dimensions={2}, use_global_device_ids=true | all-gather | bytes 6528 | tf_op jit(solution)/shard_map/all_gather | solution.py:43
  261.9 40.7 %all-gather.4 = bf16[1,2,768]{1,0,2:T(2,128)(2,1)S(1)} all-gather(bf16[1,2,48]{1,0,2:T(2,128)(2,1)} %copy.362), channel_id=6, replica_groups=mesh['dp'=16,'tensor'=2] {'dp'}, dimensions={2}, use_global_device_ids=true | all-gather | bytes 3264 | tf_op jit(solution)/shard_map/all_gather | solution.py:42
  302.6 4.6 fusion.176
  307.2 11.0 slice_reduce_fusion.4
  326.4 3.6 convolution_add_fusion.5
  330.1 3.8 fusion.121
  336.2 3.8 multiply_convert_fusion.7
  343.3 3.5 collective-permute-done.23
  347.4 4.3 collective-permute-start.24
  354.0 5.9 collective-permute-start.25
  362.1 5.9 collective-permute-start.26
  370.3 5.9 collective-permute-start.27
  377.9 6.0 collective-permute-start.28
  386.0 6.1 collective-permute-start.29
  410.7 28.1 %all-gather.29.cloned.1.call-done = bf16[1,3,768,384]{3,2,1,0:T(8,128)(2,1)} async-done(((bf16[1,3,48,384]{3,2,1,0:T(8,128)(2,1)}), bf16[1,3,768,384]{3,2,1,0:T(8,128)(2,1)}) %all-gather.29.cloned.1.call-update) | async-done | bytes 1769488 | tf_op jit(solution)/shard_map/all_gather | solution.py:36
  471.7 41.8 %all-gather.10 = bf16[1,4,768]{1,0,2:T(2,128)(2,1)S(1)} all-gather(bf16[1,4,48]{1,0,2:T(2,128)(2,1)} %copy.364), channel_id=12, replica_groups=mesh['dp'=16,'tensor'=2] {'dp'}, dimensions={2}, use_global_device_ids=true | all-gather | bytes 6528 | tf_op jit(solution)/shard_map/all_gather | solution.py:43
  513.9 40.0 %all-gather.11 = bf16[1,2,768]{1,0,2:T(2,128)(2,1)S(1)} all-gather(bf16[1,2,48]{1,0,2:T(2,128)(2,1)} %copy.365), channel_id=13, replica_groups=mesh['dp'=16,'tensor'=2] {'dp'}, dimensions={2}, use_global_device_ids=true | all-gather | bytes 3264 | tf_op jit(solution)/shard_map/all_gather | solution.py:42
  553.9 4.6 fusion.174
  558.5 11.8 slice_reduce_fusion
  575.8 3.7 convolution_add_fusion.4
  579.6 30.3 %all-gather.33.cloned.1.call-done = bf16[1,1536,768]{1,2,0:T(8,128)(2,1)} async-done(((bf16[1,1536,48]{1,2,0:T(8,128)(2,1)}), bf16[1,1536,768]{1,2,0:T(8,128)(2,1)}) %all-gather.33.cloned.1.call-update) | async-done | bytes 2359312 | tf_op jit(solution)/shard_map/all_gather | solution.py:41
  609.8 3.8 fusion.133
  616.0 3.9 multiply_convert_fusion.6
  623.7 7.9 reduce-scatter.49.cloned.1.call-done
  644.9 3.9 convert_reduce_fusion.1
  655.8 6.8 reduce-scatter.59.cloned.1.call-done
  662.6 3.4 fusion.213
  697.3 3.2 fusion.100
  710.5 3.3 fusion.103
  716.9 5.9 reduce-scatter.61.cloned.1.call-done
  736.5 3.9 convert_reduce_fusion.2
  806.3 3.0 fusion.109
  816.3 4.0 copy.318
  823.1 3.9 copy.315
  839.3 3.0 convolution_add_fusion
  844.4 3.1 convolution_add_fusion.1
  850.1 34.1 %reduce-scatter.89.cloned.1.call-done = f32[96,1]{1,0:T(8,128)} async-done(((f32[1536,1]{1,0:T(8,128)}), f32[96,1]{1,0:T(8,128)}) %reduce-scatter.89.cloned.1.call-update) | async-done | bytes 400
  885.4 125.7 %reduce-scatter.93.cloned.1.call-done = f32[48,2]{1,0:T(8,128)} async-done(((f32[768,2]{1,0:T(8,128)}), f32[48,2]{1,0:T(8,128)}) %reduce-scatter.93.cloned.1.call-update) | async-done | bytes 400
  1011.9 127.0 %reduce-scatter.87.cloned.1.call-done = f32[96,1]{1,0:T(8,128)} async-done(((f32[1536,1]{1,0:T(8,128)}), f32[96,1]{1,0:T(8,128)}) %reduce-scatter.87.cloned.1.call-update) | async-done | bytes 400
  1140.3 125.3 %reduce-scatter.97.cloned.1.call-done = f32[48,4]{1,0:T(8,128)} async-done(((f32[768,4]{1,0:T(8,128)}), f32[48,4]{1,0:T(8,128)}) %reduce-scatter.97.cloned.1.call-update) | async-done | bytes 784
  1266.7 40.4 %all-reduce.6 = (f32[2,1,384]{2,0,1:T(2,128)S(1)}, f32[2,1,384]{2,0,1:T(2,128)S(1)}) all-reduce(f32[2,1,384]{2,0,1:T(2,128)S(1)} %fusion.199, f32[2,1,384]{2,0,1:T(2,128)S(1)} %fusion.198), channel_id=53, replica_groups=mesh['dp'=16,'tensor'=2] {'dp'}, use_global_device_ids=true, to_apply=%region_73.74.clone | all-reduce | flops 1536 | bytes 12288
  1307.9 84.7 %reduce-scatter.91.cloned.1.call-done = f32[48,2]{1,0:T(8,128)} async-done(((f32[768,2]{1,0:T(8,128)}), f32[48,2]{1,0:T(8,128)}) %reduce-scatter.91.cloned.1.call-update) | async-done | bytes 400
  1393.4 126.0 %reduce-scatter.95.cloned.1.call-done = f32[48,4]{1,0:T(8,128)} async-done(((f32[768,4]{1,0:T(8,128)}), f32[48,4]{1,0:T(8,128)}) %reduce-scatter.95.cloned.1.call-update) | async-done | bytes 784
  1520.2 3.1 all-reduce.8
  1523.2 5.7 reduce-scatter.73.cloned.1.call-done
  1529.9 10.2 reduce-scatter.65.cloned.1.call-done
  1542.0 129.7 %reduce-scatter.77.cloned.1.call-done = f32[384,48]{0,1:T(8,128)} async-done(((f32[384,768]{0,1:T(8,128)}), f32[384,48]{0,1:T(8,128)}) %reduce-scatter.77.cloned.1.call-update) | async-done | bytes 73744 | tf_op jit(solution)/shard_map/reduce_scatter | solution.py:356
  1671.7 129.3 %reduce-scatter.75.cloned.1.call-done = f32[384,48]{0,1:T(8,128)} async-done(((f32[384,768]{0,1:T(8,128)}), f32[384,48]{0,1:T(8,128)}) %reduce-scatter.75.cloned.1.call-update) | async-done | bytes 73744 | tf_op jit(solution)/shard_map/reduce_scatter | solution.py:356
  1802.6 282.4 %all-reduce.12.cloned.1.call-done = (f32[3,768,384]{2,0,1:T(4,128)}, f32[3,768,384]{2,0,1:T(4,128)}) async-done(((f32[3,768,384]{2,0,1:T(4,128)}, f32[3,768,384]{2,0,1:T(4,128)}), (f32[3,768,384]{2,0,1:T(4,128)}, f32[3,768,384]{2,0,1:T(4,128)})) %all-reduce.12.cloned.1.call-update) | async-done | bytes 7077904
  2087.9 140.0 %reduce-scatter.81.cloned.1.call-done = f32[48,1536]{1,0:T(8,128)} async-done(((f32[768,1536]{1,0:T(8,128)}), f32[48,1536]{1,0:T(8,128)}) %reduce-scatter.81.cloned.1.call-update) | async-done | bytes 294928 | tf_op jit(solution)/shard_map/reduce_scatter | solution.py:357
  2227.9 143.5 %reduce-scatter.79.cloned.1.call-done = f32[48,1536]{1,0:T(8,128)} async-done(((f32[768,1536]{1,0:T(8,128)}), f32[48,1536]{1,0:T(8,128)}) %reduce-scatter.79.cloned.1.call-update) | async-done | bytes 294928 | tf_op jit(solution)/shard_map/reduce_scatter | solution.py:357
  2373.3 141.5 %reduce-scatter.85.cloned.1.call-done = f32[1536,48]{0,1:T(8,128)} async-done(((f32[1536,768]{0,1:T(8,128)}), f32[1536,48]{0,1:T(8,128)}) %reduce-scatter.85.cloned.1.call-update) | async-done | bytes 294928 | tf_op jit(solution)/shard_map/reduce_scatter | solution.py:359
  2514.8 143.1 %reduce-scatter.83.cloned.1.call-done = f32[1536,48]{0,1:T(8,128)} async-done(((f32[1536,768]{0,1:T(8,128)}), f32[1536,48]{0,1:T(8,128)}) %reduce-scatter.83.cloned.1.call-update) | async-done | bytes 294928 | tf_op jit(solution)/shard_map/reduce_scatter | solution.py:359
  (874 shorter events, 315.1 us)
Async XLA Ops:
  7.2 155.2 %all-gather.23.cloned.1.call-start = ((), (), s32[]{:S(2)}) async-start(), calls=%async_computation.44 | async-start | bytes 1880064 | tf_op jit(solution)/shard_map/all_gather | solution.py:36
  8.0 100.7 %collective-permute-start.8 = (bf16[384,48]{0,1:T(8,128)(2,1)S(1)}, bf16[384,48]{0,1:T(8,128)(2,1)S(1)}, u32[]{:S(2)}, u32[]{:S(2)}) collective-permute-start(bf16[384,48]{0,1:T(8,128)(2,1)S(1)} %get-tuple-element.419), channel_id=1, source_target_pairs={{2,0},{4,2},{6,4},{8,6},{10,8},{12,10},{14,12},{16,14},{18,16},{20... | collective-permute-start | bytes 110600 | tf_op jit(solution)/shard_map/ppermute | solution.py:27
  15.0 47.6 %collective-permute-start = (bf16[384,48]{0,1:T(8,128)(2,1)S(1)}, bf16[384,48]{0,1:T(8,128)(2,1)S(1)}, u32[]{:S(2)}, u32[]{:S(2)}) collective-permute-start(bf16[384,48]{0,1:T(8,128)(2,1)S(1)} %get-tuple-element.419), channel_id=1, source_target_pairs={{0,2},{2,4},{4,6},{6,8},{8,10},{10,12},{12,14},{14,16},{16,18},{18... | collective-permute-start | bytes 110600 | tf_op jit(solution)/shard_map/ppermute | solution.py:25
  15.1 91.9 %collective-permute-start.15 = (bf16[384,48]{0,1:T(8,128)(2,1)S(1)}, bf16[384,48]{0,1:T(8,128)(2,1)S(1)}, u32[]{:S(2)}, u32[]{:S(2)}) collective-permute-start(bf16[384,48]{0,1:T(8,128)(2,1)S(1)} %get-tuple-element.418), channel_id=1, source_target_pairs={{0,2},{2,4},{4,6},{6,8},{8,10},{10,12},{12,14},{14,16},{16,18},{18... | collective-permute-start | bytes 110600 | tf_op jit(solution)/shard_map/ppermute | solution.py:25
  16.7 301.5 %reduce-scatter.43.cloned.1.call-start = ((), (), s32[]{:S(2)}) async-start(), calls=%async_computation.28 | async-start | bytes 589824 | tf_op jit(solution)/shard_map/reduce_scatter | solution.py:52
  62.7 44.3 %collective-permute-start.1 = (bf16[384,48]{0,1:T(8,128)(2,1)S(1)}, bf16[384,48]{0,1:T(8,128)(2,1)S(1)}, u32[]{:S(2)}, u32[]{:S(2)}) collective-permute-start(bf16[384,48]{0,1:T(8,128)(2,1)S(1)} %collective-permute-done), channel_id=1, source_target_pairs={{0,2},{2,4},{4,6},{6,8},{8,10},{10,12},{12,14},{14,16},{16,18},{18... | collective-permute-start | bytes 110600 | tf_op jit(solution)/shard_map/ppermute | solution.py:25
  106.9 7.6 collective-permute-start.16
  107.0 8.0 collective-permute-start.2
  108.7 7.2 collective-permute-start.9
  114.5 7.6 collective-permute-start.17
  115.0 7.6 collective-permute-start.3
  116.0 7.6 collective-permute-start.10
  122.1 7.6 collective-permute-start.18
  122.5 7.6 collective-permute-start.4
  123.5 7.6 collective-permute-start.11
  129.6 7.6 collective-permute-start.19
  130.1 7.6 collective-permute-start.5
  131.1 8.6 collective-permute-start.12
  137.2 8.1 collective-permute-start.20
  137.6 7.7 collective-permute-start.6
  139.7 7.8 collective-permute-start.13
  145.3 7.8 collective-permute-start.21
  145.3 7.9 collective-permute-start.7
  147.5 13.4 collective-permute-start.14
  153.1 7.6 collective-permute-start.22
  171.1 148.8 %reduce-scatter.51.cloned.1.call-start = ((), (), s32[]{:S(2)}) async-start(), calls=%async_computation.32 | async-start | bytes 589824 | tf_op jit(solution)/shard_map/reduce_scatter | solution.py:52
  176.2 150.2 %all-gather.25.cloned.1.call-start = ((), (), s32[]{:S(2)}) async-start(), calls=%async_computation.45 | async-start | bytes 2506752 | tf_op jit(solution)/shard_map/all_gather | solution.py:39
  177.0 153.0 %all-gather.27.cloned.1.call-start = ((), (), s32[]{:S(2)}) async-start(), calls=%async_computation.46 | async-start | bytes 2506752 | tf_op jit(solution)/shard_map/all_gather | solution.py:41
  178.8 224.8 %reduce-scatter.53.cloned.1.call-start = ((), (), s32[]{:S(2)}) async-start(), calls=%async_computation.33 | async-start | bytes 589824 | tf_op jit(solution)/shard_map/reduce_scatter | solution.py:52
  333.8 69.8 %reduce-scatter.45.cloned.1.call-start = ((), (), s32[]{:S(2)}) async-start(), calls=%async_computation.29 | async-start | bytes 589824 | tf_op jit(solution)/shard_map/reduce_scatter | solution.py:52
  342.6 96.2 %all-gather.29.cloned.1.call-start = ((), (), s32[]{:S(2)}) async-start(), calls=%async_computation.47 | async-start | bytes 1880064 | tf_op jit(solution)/shard_map/all_gather | solution.py:36
  347.4 5.9 collective-permute-start.24
  354.0 7.6 collective-permute-start.25
  362.1 7.6 collective-permute-start.26
  370.3 7.6 collective-permute-start.27
  377.9 8.1 collective-permute-start.28
  383.9 186.4 %reduce-scatter.47.cloned.1.call-start = ((), (), s32[]{:S(2)}) async-start(), calls=%async_computation.30 | async-start | bytes 589824 | tf_op jit(solution)/shard_map/reduce_scatter | solution.py:52
  386.0 14.4 collective-permute-start.29
  458.1 112.3 %reduce-scatter.55.cloned.1.call-start = ((), (), s32[]{:S(2)}) async-start(), calls=%async_computation.34 | async-start | bytes 589824 | tf_op jit(solution)/shard_map/reduce_scatter | solution.py:52
  467.7 108.2 %all-gather.31.cloned.1.call-start = ((), (), s32[]{:S(2)}) async-start(), calls=%async_computation.48 | async-start | bytes 2506752 | tf_op jit(solution)/shard_map/all_gather | solution.py:39
  468.4 141.4 %all-gather.33.cloned.1.call-start = ((), (), s32[]{:S(2)}) async-start(), calls=%async_computation.49 | async-start | bytes 2506752 | tf_op jit(solution)/shard_map/all_gather | solution.py:41
  469.0 154.7 %reduce-scatter.57.cloned.1.call-start = ((), (), s32[]{:S(2)}) async-start(), calls=%async_computation.35 | async-start | bytes 589824 | tf_op jit(solution)/shard_map/reduce_scatter | solution.py:52
  613.6 18.0 reduce-scatter.49.cloned.1.call-start
  622.3 30.3 %reduce-scatter.67.cloned.1.call-start = ((), (), s32[]{:S(2)}) async-start(), calls=%async_computation.40 | async-start | bytes 589824 | tf_op jit(solution)/shard_map/reduce_scatter | solution.py:52
  642.5 20.1 reduce-scatter.59.cloned.1.call-start
  651.3 62.6 %reduce-scatter.69.cloned.1.call-start = ((), (), s32[]{:S(2)}) async-start(), calls=%async_computation.41 | async-start | bytes 589824 | tf_op jit(solution)/shard_map/reduce_scatter | solution.py:52
  700.6 22.2 reduce-scatter.61.cloned.1.call-start
  713.8 60.7 %reduce-scatter.63.cloned.1.call-start = ((), (), s32[]{:S(2)}) async-start(), calls=%async_computation.38 | async-start | bytes 589824 | tf_op jit(solution)/shard_map/reduce_scatter | solution.py:52
  734.1 40.4 %reduce-scatter.71.cloned.1.call-start = ((), (), s32[]{:S(2)}) async-start(), calls=%async_computation.42 | async-start | bytes 589824 | tf_op jit(solution)/shard_map/reduce_scatter | solution.py:52
  742.9 141.3 %reduce-scatter.89.cloned.1.call-start = ((), (), s32[]{:S(2)}) async-start(), calls=%async_computation.57 | async-start | bytes 835584
  751.0 260.0 %reduce-scatter.93.cloned.1.call-start = ((), (), s32[]{:S(2)}) async-start(), calls=%async_computation.59 | async-start | bytes 417792
  760.5 378.4 %reduce-scatter.87.cloned.1.call-start = ((), (), s32[]{:S(2)}) async-start(), calls=%async_computation.56 | async-start | bytes 835584
  765.0 500.6 %reduce-scatter.97.cloned.1.call-start = ((), (), s32[]{:S(2)}) async-start(), calls=%async_computation.61 | async-start | bytes 417792
  774.4 618.1 %reduce-scatter.91.cloned.1.call-start = ((), (), s32[]{:S(2)}) async-start(), calls=%async_computation.58 | async-start | bytes 417792
  794.0 725.4 %reduce-scatter.95.cloned.1.call-start = ((), (), s32[]{:S(2)}) async-start(), calls=%async_computation.60 | async-start | bytes 417792
  798.0 731.0 %reduce-scatter.73.cloned.1.call-start = ((), (), s32[]{:S(2)}) async-start(), calls=%async_computation.43 | async-start | bytes 589824 | tf_op jit(solution)/shard_map/reduce_scatter | solution.py:52
  802.3 737.8 %reduce-scatter.65.cloned.1.call-start = ((), (), s32[]{:S(2)}) async-start(), calls=%async_computation.39 | async-start | bytes 589824 | tf_op jit(solution)/shard_map/reduce_scatter | solution.py:52
  809.3 862.4 %reduce-scatter.77.cloned.1.call-start = ((), (), s32[]{:S(2)}) async-start(), calls=%async_computation.51 | async-start | bytes 1253376 | tf_op jit(solution)/shard_map/reduce_scatter | solution.py:356
  811.8 989.2 %reduce-scatter.75.cloned.1.call-start = ((), (), s32[]{:S(2)}) async-start(), calls=%async_computation.50 | async-start | bytes 1253376 | tf_op jit(solution)/shard_map/reduce_scatter | solution.py:356
  814.2 1270.8 %all-reduce.12.cloned.1.call-start = ((), (), s32[]{:S(2)}) async-start(), calls=%async_computation.62 | async-start | bytes 18874368
  827.1 1400.8 %reduce-scatter.81.cloned.1.call-start = ((), (), s32[]{:S(2)}) async-start(), calls=%async_computation.53 | async-start | bytes 5013504 | tf_op jit(solution)/shard_map/reduce_scatter | solution.py:357
  832.2 1539.2 %reduce-scatter.79.cloned.1.call-start = ((), (), s32[]{:S(2)}) async-start(), calls=%async_computation.52 | async-start | bytes 5013504 | tf_op jit(solution)/shard_map/reduce_scatter | solution.py:357
  837.3 1677.5 %reduce-scatter.85.cloned.1.call-start = ((), (), s32[]{:S(2)}) async-start(), calls=%async_computation.55 | async-start | bytes 5013504 | tf_op jit(solution)/shard_map/reduce_scatter | solution.py:359
  842.4 1815.5 %reduce-scatter.83.cloned.1.call-start = ((), (), s32[]{:S(2)}) async-start(), calls=%async_computation.54 | async-start | bytes 5013504 | tf_op jit(solution)/shard_map/reduce_scatter | solution.py:359
  (211 other events, 5350.8 us)
Sparse Core Ops, SparseCore 0:
  16.8 61.7 all-gather.22
  171.2 3.6 reduce-scatter.42
  177.7 8.9 reduce-scatter.50
  189.9 66.1 all-gather.24
  258.7 61.7 all-gather.26
  334.0 4.2 reduce-scatter.52
  342.7 7.3 reduce-scatter.44
  384.1 54.6 all-gather.28
  458.2 6.5 reduce-scatter.46
  467.8 8.5 reduce-scatter.54
  479.8 65.1 all-gather.30
  547.6 62.1 all-gather.32
  613.7 6.1 reduce-scatter.56
  622.6 8.9 reduce-scatter.48
  642.6 8.9 reduce-scatter.66
  653.7 8.9 reduce-scatter.58
  700.7 8.9 reduce-scatter.68
  713.9 8.8 reduce-scatter.60
  734.3 8.9 reduce-scatter.62
  745.3 8.9 reduce-scatter.70
  759.0 125.1 reduce-scatter.88
  888.8 122.1 reduce-scatter.92
  1015.8 123.0 reduce-scatter.86
  1143.4 122.1 reduce-scatter.96
  1270.3 122.2 reduce-scatter.90
  1397.1 122.2 reduce-scatter.94
  1522.0 6.8 reduce-scatter.72
  1531.2 8.9 reduce-scatter.64
  1544.9 126.7 reduce-scatter.76
  1676.3 124.6 reduce-scatter.74
  1807.4 277.5 all-reduce.11
  2090.2 137.6 reduce-scatter.80
  2232.9 138.4 reduce-scatter.78
  2376.6 138.1 reduce-scatter.84
  2519.9 137.9 reduce-scatter.82
